TPU v7x, 512 devices: a whole 4x4x16 slice. The times are simulated.
512 devices in a mesh: row: 32 (over x, y, core), col: 16 (over z).
Axes of the slice: x: 4, y: 4, z: 16, core: 2. Of those that a mesh axis runs over, the one named last changes fastest.
Arguments:
- features: bfloat16 [65536, 256], P('col', 'row'), may hold values from -6 to 6
- weight: bfloat16 [256, 256], replicated, may hold values from -0.375 to 0.375
- adj_values: bfloat16 [32, 16, 96, 128, 128], P('row', 'col'), may hold values from -0.0625 to 0.0625
- block_rows: int32 [32, 16, 96], P('row', 'col'), may hold values from 0 to 15, as said below
- block_cols: int32 [32, 16, 96], P('row', 'col'), may hold values from 0 to 31
- block_counts: int32 [32, 16], P('row', 'col'), may hold values from 1 to 96, as said below
- cotangent: bfloat16 [65536, 256], P(('row', 'col')), may hold values from -6 to 6
Outputs:
- output: bfloat16 [65536, 256], P(('row', 'col'))
- grad_weight: float32 [256, 256], replicated
- grad_features: bfloat16 [65536, 256], P('col', 'row')
Inputs may be any that keep to these rules, and one draw needn't show every extreme that they name: Within one tile the pairs (block_rows, block_cols) over all 96 slots are distinct. `block_counts`: some tile holds exactly 96 live blocks and some other tile exactly one in every draw.
All inputs are finite; a program needn't handle non-finite values.
Results may differ from a plain program's by a relative error of at most 0.029.
Values may be sent and summed in bfloat16 or wider, within the bound.
A program may use at most 64 MiB of HBM per device.

v0:
```python
import math
import jax
import jax.numpy as jnp
from jax import lax
from jax.sharding import PartitionSpec as P

RB = 16


def block_product(tile_values, tile_rows, tile_cols, live_count, panels, out_blocks, transposed):
    padded = tile_values.shape[0]
    blocks_turn = math.gcd(padded, 16)
    block_size = panels.shape[1]
    columns = panels.shape[2]
    turns_needed = (live_count + blocks_turn - 1) // blocks_turn

    def step(turn_index, running):
        offset = turn_index * blocks_turn
        values_now = lax.dynamic_slice_in_dim(tile_values, offset, blocks_turn, 0)
        row_ids = lax.dynamic_slice_in_dim(tile_rows, offset, blocks_turn, 0)
        col_ids = lax.dynamic_slice_in_dim(tile_cols, offset, blocks_turn, 0)
        is_live = offset + jnp.arange(blocks_turn, dtype=jnp.int32) < live_count
        if transposed:
            picked = jnp.take(panels, row_ids, axis=0)
            product = jnp.einsum(
                "bij,bif->bjf", values_now, picked, preferred_element_type=jnp.float32
            )
            target_ids = col_ids
        else:
            picked = jnp.take(panels, col_ids, axis=0)
            product = jnp.einsum(
                "bij,bjf->bif", values_now, picked, preferred_element_type=jnp.float32
            )
            target_ids = row_ids
        contribution = jnp.where(is_live[:, None, None], product, 0.0)
        return running.at[target_ids].add(contribution)

    start_sum = jnp.zeros((out_blocks, block_size, columns), jnp.float32)
    return lax.fori_loop(0, turns_needed, step, start_sum)


def shards(features, weight, adj_values, block_rows, block_cols, block_counts, cotangent):
    tile_values = adj_values[0, 0]
    tile_rows = block_rows[0, 0]
    tile_cols = block_cols[0, 0]
    live_count = block_counts[0, 0]
    block_size = tile_values.shape[1]
    col_blocks = features.shape[0] // block_size
    node_total = col_blocks * block_size * lax.axis_size("col")
    panel_part = lax.all_gather(features, "row", axis=1, tiled=True)
    panels = panel_part.reshape(col_blocks, block_size, panel_part.shape[1])
    partial_value = block_product(tile_values, tile_rows, tile_cols, live_count, panels, RB, False)
    partial_value = partial_value.reshape(RB * block_size, partial_value.shape[2])
    aggregated = lax.psum_scatter(
        partial_value.astype(jnp.bfloat16), "col", scatter_dimension=0, tiled=True
    )
    preact = jnp.dot(aggregated, weight, preferred_element_type=jnp.float32)
    output = jax.nn.silu(preact).astype(jnp.bfloat16)
    sigmoid_pre = jax.nn.sigmoid(preact)
    slopes = sigmoid_pre * (1.0 + preact * (1.0 - sigmoid_pre))
    deltas = (cotangent.astype(jnp.float32) * slopes).astype(jnp.bfloat16)
    local_grad = jnp.dot(aggregated.T, deltas, preferred_element_type=jnp.float32)
    grad_weight = lax.psum(local_grad, ("row", "col")) * (1.0 / math.sqrt(node_total))
    backward = jnp.dot(deltas, weight.T, preferred_element_type=jnp.float32).astype(jnp.bfloat16)
    back_slab = lax.all_gather(backward, "col", axis=0, tiled=True)
    back_panels = back_slab.reshape(RB, block_size, back_slab.shape[1])
    column_terms = block_product(
        tile_values, tile_rows, tile_cols, live_count, back_panels, col_blocks, True
    )
    column_terms = column_terms.reshape(col_blocks * block_size, column_terms.shape[2])
    grad_features = lax.psum_scatter(
        column_terms.astype(jnp.bfloat16), "row", scatter_dimension=1, tiled=True
    )
    return (output, grad_weight, grad_features)


def solution(mesh):
    return jax.shard_map(
        shards,
        mesh=mesh,
        in_specs=(
            P("col", "row"),
            P(),
            P("row", "col", None, None, None),
            P("row", "col", None),
            P("row", "col", None),
            P("row", "col"),
            P(("row", "col"), None),
        ),
        out_specs=(P(("row", "col"), None), P(), P("col", "row")),
        check_vma=False,
    )
```

profile of v0, /device:TPU:2, one launch (start us, length us, event | category | flops | bytes accessed | tf_op | source)
XLA Modules:
  0.0 847.8 jit_solution(3140927563884392423)
XLA Ops:
  8.6 65.7 %all-gather.3.cloned.1.call-done = bf16[4096,256]{0,1:T(8,128)(2,1)} async-done(((bf16[4096,8]{0,1:T(8,128)(2,1)}), bf16[4096,256]{0,1:T(8,128)(2,1)}) %all-gather.3.cloned.1.call-update) | async-done | bytes 2097168 | tf_op jit(solution)/shard_map/all_gather | solution.py:50
  74.3 4.1 copy.11
  78.4 1.5 broadcast_in_dim.58
  80.0 35.9 %while.20 = (s32[]{:T(128)}, f32[16,128,256]{2,1,0:T(8,128)}, s32[]{:T(128)}, s32[96]{0:T(128)S(1)}, s32[]{:T(128)}, /*index=5*/bf16[96,128,128]{2,1,0:T(8,128)(...) while((s32[]{:T(128)}, f32[16,128,256]{2,1,0:T(8,128)}, ...), condition=%wide.region_2.3_spmd, body=%wide.region_0.2_spmd.sunk | while | flops 135791792 | bytes 12063415 | solution.py:39
  80.0 0.7 compare_and_fusion.4
  80.7 2.2 gather_fusion
  82.9 1.5 convolution_select_fusion.4
  84.5 4.3 scatter_fusion
  88.9 0.7 compare_and_fusion.4
  89.6 2.2 gather_fusion
  91.8 1.6 convolution_select_fusion.4
  93.4 4.4 scatter_fusion
  97.8 0.7 compare_and_fusion.4
  98.5 2.2 gather_fusion
  100.8 1.5 convolution_select_fusion.4
  102.4 4.5 scatter_fusion
  106.8 0.7 compare_and_fusion.4
  107.6 2.2 gather_fusion
  109.8 1.6 convolution_select_fusion.4
  111.4 4.4 scatter_fusion
  115.9 2.8 convert_element_type.24
  118.8 87.5 %reduce-scatter.3.cloned.1.call-done = bf16[128,256]{1,0:T(8,128)(2,1)} async-done(((bf16[2048,256]{1,0:T(8,128)(2,1)}), bf16[128,256]{1,0:T(8,128)(2,1)}) %reduce-scatter.3.cloned.1.call-update) | async-done | bytes 65552 | tf_op jit(solution)/shard_map/reduce_scatter | solution.py:54
  206.3 1.7 multiply_convert_fusion
  208.0 0.8 convolution_convert_fusion
  208.9 2.8 copy.10
  211.7 0.9 fusion.12
  212.7 65.3 %all-gather.5.cloned.1.call-done = bf16[2048,256]{1,0:T(8,128)(2,1)} async-done(((bf16[128,256]{1,0:T(8,128)(2,1)}), bf16[2048,256]{1,0:T(8,128)(2,1)}) %all-gather.5.cloned.1.call-update) | async-done | bytes 1048592 | tf_op jit(solution)/shard_map/all_gather | solution.py:65
  278.1 2.4 broadcast_in_dim.59
  280.5 34.6 %while.21 = (s32[]{:T(128)}, f32[32,128,256]{2,1,0:T(8,128)}, s32[]{:T(128)}, s32[96]{0:T(128)S(1)}, s32[]{:T(128)}, /*index=5*/bf16[96,128,128]{1,2,0:T(8,128)(...) while((s32[]{:T(128)}, f32[32,128,256]{2,1,0:T(8,128)}, ...), condition=%wide.region_7.8_spmd, body=%wide.region_5.7_spmd.sunk | while | flops 135791792 | bytes 12063415 | solution.py:39
  281.2 1.8 gather_fusion.1
  283.1 1.6 convolution_select_fusion.5
  284.7 4.3 scatter_fusion.1
  289.8 1.8 gather_fusion.1
  291.6 1.5 convolution_select_fusion.5
  293.3 4.5 scatter_fusion.1
  297.7 0.7 compare_and_fusion.5
  298.5 1.8 gather_fusion.1
  300.3 1.6 convolution_select_fusion.5
  301.9 4.5 scatter_fusion.1
  306.4 0.7 compare_and_fusion.5
  307.1 1.8 gather_fusion.1
  309.0 1.6 convolution_select_fusion.5
  310.6 4.4 scatter_fusion.1
  315.1 2.5 convert_element_type.30
  317.6 2.9 copy.15
  320.5 418.5 %all-reduce.2.cloned.1.call-done = f32[256,256]{1,0:T(8,128)} async-done(((f32[256,256]{1,0:T(8,128)}), f32[256,256]{1,0:T(8,128)}) %all-reduce.2.cloned.1.call-update) | async-done | bytes 262160 | tf_op jit(solution)/shard_map/psum | solution.py:63
  739.0 1.7 broadcast_multiply_fusion
  740.6 100.6 %reduce-scatter.5.cloned.1.call-done = bf16[4096,8]{0,1:T(8,128)(2,1)} async-done(((bf16[4096,256]{0,1:T(8,128)(2,1)}), bf16[4096,8]{0,1:T(8,128)(2,1)}) %reduce-scatter.5.cloned.1.call-update) | async-done | bytes 65552 | tf_op jit(solution)/shard_map/reduce_scatter | solution.py:71
  (40 shorter events, 3.1 us)
Async XLA Ops:
  7.2 199.1 %copy-start = (bf16[256,256]{1,0:T(8,128)(2,1)S(1)}, bf16[256,256]{1,0:T(8,128)(2,1)}, u32[]{:S(2)}) copy-start(bf16[256,256]{1,0:T(8,128)(2,1)} %param.12) | copy-start | bytes 393220
  7.2 67.2 %all-gather.3.cloned.1.call-start = ((), (), s32[]{:S(2)}) async-start(), calls=%async_computation.2 | async-start | bytes 2162688 | tf_op jit(solution)/shard_map/all_gather | solution.py:50
  7.9 198.4 %reduce-scatter.3.cloned.1.call-start = ((), (), s32[]{:S(2)}) async-start(), calls=%async_computation.3 | async-start | bytes 1114112 | tf_op jit(solution)/shard_map/reduce_scatter | solution.py:54
  78.4 1.5 copy-start.3
  78.4 1.5 copy-start.4
  115.9 90.4 %copy-start.5 = (bf16[128,256]{1,0:T(8,128)(2,1)S(1)}, bf16[128,256]{1,0:T(8,128)(2,1)}, u32[]{:S(2)}) copy-start(bf16[128,256]{1,0:T(8,128)(2,1)} %param.17) | copy-start | bytes 196612
  115.9 93.1 %copy-start.1 = (bf16[96,128,128]{2,1,0:T(8,128)(2,1)S(1)}, bf16[96,128,128]{2,1,0:T(8,128)(2,1)}, u32[]{:S(2)}) copy-start(bf16[96,128,128]{2,1,0:T(8,128)(2,1)} %get-tuple-element.328) | copy-start | bytes 9437188
  118.7 159.3 %all-gather.5.cloned.1.call-start = ((), (), s32[]{:S(2)}) async-start(), calls=%async_computation.5 | async-start | bytes 1114112 | tf_op jit(solution)/shard_map/all_gather | solution.py:65
  208.9 2.9 copy-start.2
  208.9 530.1 %all-reduce.2.cloned.1.call-start = ((), (), s32[]{:S(2)}) async-start(), calls=%async_computation.4 | async-start | bytes 524288 | tf_op jit(solution)/shard_map/psum | solution.py:63
  212.7 628.6 %reduce-scatter.5.cloned.1.call-start = ((), (), s32[]{:S(2)}) async-start(), calls=%async_computation.6 | async-start | bytes 2162688 | tf_op jit(solution)/shard_map/reduce_scatter | solution.py:71
Sparse Core Ops, SparseCore 0:
  11.1 63.1 all-gather.2
  118.9 87.4 reduce-scatter.2
  209.2 68.8 all-gather.4
  284.8 454.1 all-reduce.1
  743.8 97.3 reduce-scatter.4
where the time goes:
time: 850 us; the launch traced here: 848 us
  waiting for transfers between devices  738 us (87%)
  other arithmetic  48.7 us (6%)
  local copies, waits for them, and re-layouts  30 us (4%)
  matrix products  15.8 us (2%)
  between operations  14.5 us (2%)
    psum x1, waiting for transfers between devices, shards(): lax.psum(local_grad, ('row', 'col')) * (1.0 / math.sqrt(node_total))  418 us
    reduce_scatter x1, waiting for transfers between devices, shards(): lax.psum_scatter(column_terms.astype(jnp.bfloat16), 'row', scatter_dimens...  101 us
    reduce_scatter x1, waiting for transfers between devices, shards(): lax.psum_scatter(partial_value.astype(jnp.bfloat16), 'col', scatter_dimen...  87.5 us
    all_gather x1, waiting for transfers between devices, shards(): panel_part = lax.all_gather(features, 'row', axis=1, tiled=True)  65.7 us
    all_gather x1, waiting for transfers between devices, shards(): back_slab = lax.all_gather(backward, 'col', axis=0, tiled=True)  65.3 us
    scatter-add x8, other arithmetic, step(): return running.at[target_ids].add(contribution)  35.2 us
  transfers between devices with their start and end apart: 5, of which 5 were waited for; matrix products, arithmetic and copies ran while one was open for 6% of the time, Pallas kernels for 0%

commit v1 on v0

--- a/solution.py
+++ b/solution.py
@@ -60,7 +60,7 @@
     slopes = sigmoid_pre * (1.0 + preact * (1.0 - sigmoid_pre))
     deltas = (cotangent.astype(jnp.float32) * slopes).astype(jnp.bfloat16)
     local_grad = jnp.dot(aggregated.T, deltas, preferred_element_type=jnp.float32)
-    grad_weight = lax.psum(local_grad, ("row", "col")) * (1.0 / math.sqrt(node_total))
+    grad_weight = lax.psum(lax.psum(local_grad, "col"), "row") * (1.0 / math.sqrt(node_total))
     backward = jnp.dot(deltas, weight.T, preferred_element_type=jnp.float32).astype(jnp.bfloat16)
     back_slab = lax.all_gather(backward, "col", axis=0, tiled=True)
     back_panels = back_slab.reshape(RB, block_size, back_slab.shape[1])

time: 850 us -> 661 us (0.78)
  waiting for transfers between devices: 738 us -> 549 us
    psum x1 -> x2, waiting for transfers between devices: 418 us -> 219 us  [the longest x1 130 us: shards(): lax.psum(local_grad, 'col')]
  transfers between devices with their start and end apart: 5 -> 6, of which waited for: 5 -> 6; matrix products, arithmetic and copies ran while one was open for 6% -> 7% of each run, Pallas kernels for 0% -> 0%
where the time goes in v1:
time: 661 us; the launch traced here: 660 us
  waiting for transfers between devices  549 us (83%)
  other arithmetic  48.9 us (7%)
  local copies, waits for them, and re-layouts  30 us (5%)
  matrix products  16.7 us (3%)
  between operations  14.8 us (2%)
    psum x1, waiting for transfers between devices, shards(): lax.psum(local_grad, 'col')  130 us
    reduce_scatter x1, waiting for transfers between devices, shards(): lax.psum_scatter(column_terms.astype(jnp.bfloat16), 'row', scatter_dimens...  106 us
    psum x1, waiting for transfers between devices, shards(): lax.psum(lax.psum(local_grad, 'col'), 'row') * (1.0 / math.sqrt(node_total))  89 us
    reduce_scatter x1, waiting for transfers between devices, shards(): lax.psum_scatter(partial_value.astype(jnp.bfloat16), 'col', scatter_dimen...  87.6 us
    all_gather x1, waiting for transfers between devices, shards(): back_slab = lax.all_gather(backward, 'col', axis=0, tiled=True)  70.4 us
    all_gather x1, waiting for transfers between devices, shards(): panel_part = lax.all_gather(features, 'row', axis=1, tiled=True)  65.7 us
    scatter-add x8, other arithmetic, step(): return running.at[target_ids].add(contribution)  35.4 us
  transfers between devices with their start and end apart: 6, of which 6 were waited for; matrix products, arithmetic and copies ran while one was open for 7% of the time, Pallas kernels for 0%

profile of v1, /device:TPU:2, one launch (start us, length us, event | category | flops | bytes accessed | tf_op | source)
XLA Modules:
  0.0 659.6 jit_solution(5772086557648280872)
XLA Ops:
  8.6 65.7 %all-gather.3.cloned.1.call-done = bf16[4096,256]{0,1:T(8,128)(2,1)} async-done(((bf16[4096,8]{0,1:T(8,128)(2,1)}), bf16[4096,256]{0,1:T(8,128)(2,1)}) %all-gather.3.cloned.1.call-update) | async-done | bytes 2097168 | tf_op jit(solution)/shard_map/all_gather | solution.py:50
  74.3 4.1 copy.11
  78.4 1.5 broadcast_in_dim.58
  80.0 36.0 %while.20 = (s32[]{:T(128)}, f32[16,128,256]{2,1,0:T(8,128)}, s32[]{:T(128)}, s32[96]{0:T(128)S(1)}, s32[]{:T(128)}, /*index=5*/bf16[96,128,128]{2,1,0:T(8,128)(...) while((s32[]{:T(128)}, f32[16,128,256]{2,1,0:T(8,128)}, ...), condition=%wide.region_2.3_spmd, body=%wide.region_0.2_spmd.sunk | while | flops 135791792 | bytes 12063415 | solution.py:39
  80.0 0.7 compare_and_fusion.4
  80.7 2.2 gather_fusion
  82.9 1.6 convolution_select_fusion.4
  84.6 4.3 scatter_fusion
  88.9 0.7 compare_and_fusion.4
  89.6 2.2 gather_fusion
  91.8 1.6 convolution_select_fusion.4
  93.5 4.4 scatter_fusion
  97.9 0.7 compare_and_fusion.4
  98.6 2.2 gather_fusion
  100.8 1.5 convolution_select_fusion.4
  102.4 4.5 scatter_fusion
  107.6 2.2 gather_fusion
  109.8 1.6 convolution_select_fusion.4
  111.5 4.5 scatter_fusion
  115.9 2.8 convert_element_type.24
  118.9 87.6 %reduce-scatter.3.cloned.1.call-done = bf16[128,256]{1,0:T(8,128)(2,1)} async-done(((bf16[2048,256]{1,0:T(8,128)(2,1)}), bf16[128,256]{1,0:T(8,128)(2,1)}) %reduce-scatter.3.cloned.1.call-update) | async-done | bytes 65552 | tf_op jit(solution)/shard_map/reduce_scatter | solution.py:54
  206.5 1.7 multiply_convert_fusion
  208.2 1.8 fusion.12
  210.0 0.8 convolution_convert_fusion
  210.9 2.8 copy.10
  213.7 129.5 %all-reduce.3.cloned.1.call-done = f32[256,256]{1,0:T(8,128)} async-done(((f32[256,256]{1,0:T(8,128)}), f32[256,256]{1,0:T(8,128)}) %all-reduce.3.cloned.1.call-update) | async-done | bytes 262160 | tf_op jit(solution)/shard_map/psum | solution.py:63
  343.4 70.4 %all-gather.5.cloned.1.call-done = bf16[2048,256]{1,0:T(8,128)(2,1)} async-done(((bf16[128,256]{1,0:T(8,128)(2,1)}), bf16[2048,256]{1,0:T(8,128)(2,1)}) %all-gather.5.cloned.1.call-update) | async-done | bytes 1048592 | tf_op jit(solution)/shard_map/all_gather | solution.py:65
  413.7 2.4 broadcast_in_dim.59
  416.2 34.6 %while.21 = (s32[]{:T(128)}, f32[32,128,256]{2,1,0:T(8,128)}, s32[]{:T(128)}, s32[96]{0:T(128)S(1)}, s32[]{:T(128)}, /*index=5*/bf16[96,128,128]{1,2,0:T(8,128)(...) while((s32[]{:T(128)}, f32[32,128,256]{2,1,0:T(8,128)}, ...), condition=%wide.region_8.9_spmd, body=%wide.region_6.8_spmd.sunk | while | flops 135791792 | bytes 12063415 | solution.py:39
  416.9 1.8 gather_fusion.1
  418.7 1.5 convolution_select_fusion.5
  420.4 4.3 scatter_fusion.1
  425.5 1.8 gather_fusion.1
  427.3 1.6 convolution_select_fusion.5
  428.9 4.5 scatter_fusion.1
  433.4 0.7 compare_and_fusion.5
  434.1 1.8 gather_fusion.1
  436.0 1.6 convolution_select_fusion.5
  437.6 4.5 scatter_fusion.1
  442.1 0.7 compare_and_fusion.5
  442.9 1.8 gather_fusion.1
  444.7 1.6 convolution_select_fusion.5
  446.4 4.5 scatter_fusion.1
  450.8 2.5 convert_element_type.30
  453.3 3.0 copy.15
  456.3 89.0 %all-reduce.5.cloned.1.call-done = f32[256,256]{1,0:T(8,128)} async-done(((f32[256,256]{1,0:T(8,128)}), f32[256,256]{1,0:T(8,128)}) %all-reduce.5.cloned.1.call-update) | async-done | bytes 262160 | tf_op jit(solution)/shard_map/psum | solution.py:63
  545.3 1.7 broadcast_multiply_fusion
  547.0 105.7 %reduce-scatter.5.cloned.1.call-done = bf16[4096,8]{0,1:T(8,128)(2,1)} async-done(((bf16[4096,256]{0,1:T(8,128)(2,1)}), bf16[4096,8]{0,1:T(8,128)(2,1)}) %reduce-scatter.5.cloned.1.call-update) | async-done | bytes 65552 | tf_op jit(solution)/shard_map/reduce_scatter | solution.py:71
  (41 shorter events, 3.9 us)
Async XLA Ops:
  7.2 199.3 %copy-start = (bf16[256,256]{1,0:T(8,128)(2,1)S(1)}, bf16[256,256]{1,0:T(8,128)(2,1)}, u32[]{:S(2)}) copy-start(bf16[256,256]{1,0:T(8,128)(2,1)} %param.12) | copy-start | bytes 393220
  7.2 67.2 %all-gather.3.cloned.1.call-start = ((), (), s32[]{:S(2)}) async-start(), calls=%async_computation.2 | async-start | bytes 2162688 | tf_op jit(solution)/shard_map/all_gather | solution.py:50
  7.9 198.6 %reduce-scatter.3.cloned.1.call-start = ((), (), s32[]{:S(2)}) async-start(), calls=%async_computation.3 | async-start | bytes 1114112 | tf_op jit(solution)/shard_map/reduce_scatter | solution.py:54
  78.4 1.5 copy-start.2
  78.4 1.5 copy-start.3
  115.9 90.6 %copy-start.4 = (bf16[128,256]{1,0:T(8,128)(2,1)S(1)}, bf16[128,256]{1,0:T(8,128)(2,1)}, u32[]{:S(2)}) copy-start(bf16[128,256]{1,0:T(8,128)(2,1)} %param.17) | copy-start | bytes 196612
  115.9 95.0 %copy-start.1 = (bf16[96,128,128]{2,1,0:T(8,128)(2,1)S(1)}, bf16[96,128,128]{2,1,0:T(8,128)(2,1)}, u32[]{:S(2)}) copy-start(bf16[96,128,128]{2,1,0:T(8,128)(2,1)} %get-tuple-element.329) | copy-start | bytes 9437188
  118.8 224.5 %all-reduce.3.cloned.1.call-start = ((), (), s32[]{:S(2)}) async-start(), calls=%async_computation.4 | async-start | bytes 524288 | tf_op jit(solution)/shard_map/psum | solution.py:63
  210.0 203.8 %all-gather.5.cloned.1.call-start = ((), (), s32[]{:S(2)}) async-start(), calls=%async_computation.6 | async-start | bytes 1114112 | tf_op jit(solution)/shard_map/all_gather | solution.py:65
  210.9 334.5 %all-reduce.5.cloned.1.call-start = ((), (), s32[]{:S(2)}) async-start(), calls=%async_computation.5 | async-start | bytes 524288 | tf_op jit(solution)/shard_map/psum | solution.py:63
  343.3 309.4 %reduce-scatter.5.cloned.1.call-start = ((), (), s32[]{:S(2)}) async-start(), calls=%async_computation.7 | async-start | bytes 2162688 | tf_op jit(solution)/shard_map/reduce_scatter | solution.py:71
Sparse Core Ops, SparseCore 0:
  11.1 63.1 all-gather.2
  118.9 87.5 reduce-scatter.2
  210.1 133.1 all-reduce.2
  345.8 67.8 all-gather.4
  416.8 128.4 all-reduce.4
  550.8 101.8 reduce-scatter.4
